TPU v7x, 256 devices: a whole 4x4x8 slice. The times are simulated.
256 devices in a mesh: ctx: 16 (over z, x_hi), fsdp: 16 (over x_lo, y, core).
Axes of the slice: x: 4 (x_hi: 2, x_lo: 2; x = x_hi * 2 + x_lo), y: 4, z: 8, core: 2. Of those that a mesh axis runs over, the one named last changes fastest.
Arguments:
- out_grad: bfloat16 [2048, 8192], P('ctx', 'fsdp'), may hold values from -6 to 6
- out_weight: bfloat16 [8192, 8192], P('ctx', 'fsdp'), may hold values from -0.0625 to 0.0625
- projections: bfloat16 [3, 2048, 8192], P(None, 'ctx', 'fsdp'), may hold values from -6 to 6
- short_filters: float32 [3, 3, 8192], P(None, None, 'fsdp'), may hold values from -3 to 3
- residues: float32 [16, 8192], P(None, 'fsdp'), may hold values from -0.06 to 0.06
- decay_rates: float32 [16, 8192], P(None, 'fsdp'), may hold values from 4.8828126e-05 to 0.05
Outputs:
- grad_weight: bfloat16 [8192, 8192], P('ctx', 'fsdp')
- grad_projections: bfloat16 [3, 2048, 8192], P(None, 'ctx', 'fsdp')
- grad_short: float32 [3, 3, 8192], P(None, None, 'fsdp')
- grad_residues: float32 [16, 8192], P(None, 'fsdp')
- grad_rates: float32 [16, 8192], P(None, 'fsdp')
All inputs are finite; a program needn't handle non-finite values.
Results may differ from a plain program's by a relative error of at most 0.005.
Values may be sent and summed in bfloat16 or wider, within the bound.
No kernel may reach another device: no remote copies, remote signals or barrier semaphores. Data moves between devices by JAX's collectives and lax.ppermute only.
A program may use at most 128 MiB of HBM per device.

v0:
```python
import math
import jax
import jax.numpy as jnp
from jax import lax
from jax.sharding import PartitionSpec as P


def from_behind(block, axis, distance):
    devices = range(lax.axis_size(axis))
    route = [(i - distance, i) for i in devices if i - distance in devices]
    return lax.ppermute(block, axis, route)


def carried_in(array, axis, combine, identity, reverse):
    devices, index = (lax.axis_size(axis), lax.axis_index(axis))
    everything = jax.tree.map(lambda part: lax.all_gather(part, axis), array)
    start = jax.tree.map(
        lambda part, zero: jnp.broadcast_to(jnp.asarray(zero, part.dtype), part.shape),
        array,
        identity,
    )

    def lap(k, before):
        at = devices - 1 - k if reverse else k
        reached = at > index if reverse else at < index
        new = combine(before, jax.tree.map(lambda part: part[at], everything))
        return jax.tree.map(lambda a, b: jnp.where(reached, a, b), new, before)

    return lax.fori_loop(0, devices, lap, start)


def link(earlier, later):
    return (earlier[0] * later[0], later[0] * earlier[1] + later[1])


def local_scan(decay, values):
    length = values.shape[0]
    piece_len = math.gcd(length, 32)
    block_count = length // piece_len
    grouped = values.reshape((block_count, piece_len) + values.shape[1:])
    running = jnp.zeros((block_count,) + decay.shape, jnp.float32)
    outputs = []
    for offset in range(piece_len):
        running = decay * running + grouped[:, offset]
        outputs.append(running)
    inner = jnp.stack(outputs, axis=1)
    jump = jnp.power(decay, float(piece_len))

    def carry_step(carry, final):
        return (jump * carry + final, carry)

    _, entering = lax.scan(carry_step, jnp.zeros(decay.shape, jnp.float32), inner[:, -1])
    steps_in = jnp.arange(piece_len, dtype=jnp.float32) + 1.0
    rising = jnp.power(decay[None], steps_in[:, None, None])
    whole = inner + rising[None] * entering[:, None]
    return whole.reshape((length,) + decay.shape)


def on_device(out_grad, out_weight, projections, short_filters, residues, decay_rates):
    panels = lax.all_gather(out_grad, "fsdp", axis=1, tiled=True)
    length = out_grad.shape[0]
    columns = panels
    grad_y = jnp.dot(
        columns,
        lax.all_gather(out_weight, "ctx", axis=0, tiled=True),
        preferred_element_type=jnp.float32,
    )
    taps = short_filters.shape[1]
    margin = taps - 1
    before = from_behind(projections[:, length - margin :, :], "ctx", 1)
    extended = jnp.concatenate([before, projections], axis=1).astype(jnp.float32)
    branches = short_filters[:, 0, None, :] * extended[:, margin : margin + length, :]
    for offset in range(1, taps):
        branches = (
            branches
            + short_filters[:, offset, None, :]
            * extended[:, margin - offset : margin - offset + length, :]
        )
    q_branch, k_branch, v_branch = (branches[0], branches[1], branches[2])
    product_kv = k_branch * v_branch
    decay = jnp.exp(-decay_rates)
    block_decay = jnp.exp(-decay_rates * float(length))
    positions = jnp.arange(length, dtype=jnp.float32)
    states_local = local_scan(decay, product_kv[:, None, :])
    identity = (jnp.ones_like(decay), jnp.zeros_like(decay))
    state_in = carried_in((block_decay, states_local[-1]), "ctx", link, identity, False)[1]
    rising = jnp.exp(-decay_rates[None] * (positions + 1.0)[:, None, None])
    states = states_local + rising * state_in[None]
    long_out = jnp.sum(residues[None] * states, axis=1)
    y_rounded = (q_branch * long_out).astype(jnp.bfloat16)
    grad_long = grad_y * q_branch
    grad_q = grad_y * long_out
    flipped = jnp.flip(grad_long, axis=0)
    adjoint_local = jnp.flip(local_scan(decay, residues[None] * flipped[:, None, :]), axis=0)
    adjoint_in = carried_in((block_decay, adjoint_local[0]), "ctx", link, identity, True)[1]
    falling = jnp.exp(-decay_rates[None] * (float(length) - positions)[:, None, None])
    adjoint = adjoint_local + falling * adjoint_in[None]
    grad_kv = jnp.sum(adjoint, axis=1)
    grad_res_part = jnp.sum(grad_long[:, None, :] * states, axis=0)
    previous = jnp.concatenate([state_in[None], states[:-1]], axis=0)
    grad_rate_part = -decay * jnp.sum(adjoint * previous, axis=0)
    grad_branches = jnp.stack([grad_q, grad_kv * v_branch, grad_kv * k_branch])
    after = from_behind(grad_branches[:, :margin, :], "ctx", -1)
    extended_back = jnp.concatenate([grad_branches, after], axis=1)
    grad_raw = short_filters[:, 0, None, :] * extended_back[:, 0:length, :]
    filter_terms = [jnp.sum(grad_branches * extended[:, margin : margin + length, :], axis=1)]
    for offset in range(1, taps):
        grad_raw = (
            grad_raw
            + short_filters[:, offset, None, :] * extended_back[:, offset : offset + length, :]
        )
        filter_terms.append(
            jnp.sum(
                grad_branches * extended[:, margin - offset : margin - offset + length, :], axis=1
            )
        )
    filter_part = jnp.stack(filter_terms, axis=1)
    grad_short, grad_res, grad_rate = lax.psum((filter_part, grad_res_part, grad_rate_part), "ctx")
    columns = panels
    grad_weight = lax.psum_scatter(
        lax.dot_general(
            columns, y_rounded, (((0,), (0,)), ((), ())), preferred_element_type=jnp.float32
        ),
        "ctx",
        scatter_dimension=0,
        tiled=True,
    )
    return (
        grad_weight.astype(jnp.bfloat16),
        grad_raw.astype(jnp.bfloat16),
        grad_short,
        grad_res,
        grad_rate,
    )


def solution(mesh):
    placed = (
        P("ctx", "fsdp"),
        P("ctx", "fsdp"),
        P(None, "ctx", "fsdp"),
        P(None, None, "fsdp"),
        P(None, "fsdp"),
        P(None, "fsdp"),
    )
    return jax.shard_map(
        on_device,
        mesh=mesh,
        in_specs=placed,
        out_specs=(
            P("ctx", "fsdp"),
            P(None, "ctx", "fsdp"),
            P(None, None, "fsdp"),
            P(None, "fsdp"),
            P(None, "fsdp"),
        ),
        check_vma=False,
    )
```

profile of v0, /device:TPU:1, one launch (start us, length us, event | category | flops | bytes accessed | tf_op | source)
XLA Modules:
  0.0 870.1 jit_solution(4104952560245108531)
XLA Ops:
  9.4 5.5 collective-permute-start
  18.4 39.6 %all-gather = f32[256,512]{1,0:T(8,128)} all-gather(f32[16,512]{1,0:T(8,128)S(1)} %get-tuple-element.508), channel_id=2, replica_groups=mesh['ctx'=16,'fsdp'=16] {'ctx'}, dimensions={0}, use_global_device_ids=true | all-gather | bytes 557056 | tf_op jit(solution)/shard_map/all_gather | solution.py:16
  58.0 1.8 broadcast_power_fusion
  68.7 119.7 %all-gather.6.cloned.1.call-done = bf16[8192,512]{1,0:T(8,128)(2,1)} async-done(((bf16[512,512]{1,0:T(8,128)(2,1)}), bf16[8192,512]{1,0:T(8,128)(2,1)}) %all-gather.6.cloned.1.call-update) | async-done | bytes 8388624 | tf_op jit(solution)/shard_map/all_gather | solution.py:65
  188.4 5.3 fusion.8
  202.1 1.6 constant_dynamic-update-slice_fusion.60
  203.7 1.7 constant_dynamic-update-slice_fusion.59
  205.3 1.6 constant_dynamic-update-slice_fusion.58
  206.9 1.7 constant_dynamic-update-slice_fusion.57
  210.1 1.6 constant_dynamic-update-slice_fusion.55
  213.4 1.6 constant_dynamic-update-slice_fusion.53
  215.0 1.6 constant_dynamic-update-slice_fusion.52
  216.6 1.7 constant_dynamic-update-slice_fusion.51
  219.8 1.7 constant_dynamic-update-slice_fusion.49
  221.5 1.6 constant_dynamic-update-slice_fusion.48
  223.0 1.7 constant_dynamic-update-slice_fusion.47
  224.7 1.6 constant_dynamic-update-slice_fusion.46
  226.3 1.7 constant_dynamic-update-slice_fusion.45
  228.0 1.6 constant_dynamic-update-slice_fusion.44
  229.5 1.7 constant_dynamic-update-slice_fusion.43
  231.2 1.6 constant_dynamic-update-slice_fusion.42
  232.8 1.7 constant_dynamic-update-slice_fusion.41
  234.5 1.6 constant_dynamic-update-slice_fusion.40
  236.1 1.6 constant_dynamic-update-slice_fusion.39
  237.7 1.6 constant_dynamic-update-slice_fusion.38
  239.3 1.7 constant_dynamic-update-slice_fusion.37
  241.0 1.6 constant_dynamic-update-slice_fusion.36
  242.6 1.7 constant_dynamic-update-slice_fusion.35
  244.3 1.6 constant_dynamic-update-slice_fusion.34
  245.9 1.7 constant_dynamic-update-slice_fusion.33
  247.6 1.7 constant_dynamic-update-slice_fusion.32
  254.9 1.7 constant_dynamic-update-slice_fusion.31
  265.3 5.6 while.58
  270.9 7.2 multiply_add_fusion.1
  280.1 2.0 copy-done.5
  282.1 32.5 %all_gather.22 = f32[16,16,512]{2,1,0:T(8,128)S(1)} all-gather(f32[1,16,512]{2,1,0:T(8,128)S(1)} %slice.365), channel_id=1, replica_groups=mesh['ctx'=16,'fsdp'=16] {'ctx'}, dimensions={0}, use_global_device_ids=true | all-gather | bytes 557056 | tf_op jit(solution)/shard_map/all_gather | solution.py:16
  314.7 12.7 %while.57 = (s32[]{:T(128)}, f32[16,512]{1,0:T(8,128)S(1)}, s32[]{:T(128)}, f32[16,16,512]{2,1,0:T(8,128)}, f32[16,16,512]{2,1,0:T(8,128)S(1)}, /*index=5*/s32[]{:T(128)}, s32[]{:T(128)}) while((s32[]{:T(128)}, f32[16,512]{1,0:T(8,128)S(1)}, s32[]{:T(128)}, f32[16,16,512]{2,1,0:T(8,128)}, f32[16,16,512]{2,1,0:T(8,128)S(1)}, ...), condition=%wide.region_3.4_spmd.clone, body=%wide.region_2.3_spmd.clone.sunk | while | flops 32772 | bytes 131173 | solution.py:29
  327.4 2.6 copy.25
  330.1 2.1 copy-done.3
  332.1 34.7 %all_gather.25 = f32[16,16,512]{2,1,0:T(8,128)S(1)} all-gather(f32[1,16,512]{2,1,0:T(8,128)S(1)} %slice.398), channel_id=1, replica_groups=mesh['ctx'=16,'fsdp'=16] {'ctx'}, dimensions={0}, use_global_device_ids=true | all-gather | bytes 557056 | tf_op jit(solution)/shard_map/all_gather | solution.py:16
  366.9 12.8 %while.59 = (s32[]{:T(128)}, f32[16,512]{1,0:T(8,128)S(1)}, s32[]{:T(128)}, f32[16,16,512]{2,1,0:T(8,128)}, f32[16,16,512]{2,1,0:T(8,128)S(1)}, /*index=5*/s32[]{:T(128)}, s32[]{:T(128)}, s32[]{:T(128)}, s32[]{:T(128)}) while((s32[]{:T(128)}, f32[16,512]{1,0:T(8,128)S(1)}, s32[]{:T(128)}, f32[16,16,512]{2,1,0:T(8,128)}, ...), condition=%wide.region_9.10_spmd.clone, body=%wide.region_8.9_spmd.clone.sunk | while | flops 32776 | bytes 131235 | solution.py:29
  379.7 3.1 slice_add_fusion
  383.2 2.3 fusion.2
  385.8 2.5 multiply_reduce_fusion
  390.6 4.0 collective-permute-done.1
  396.7 8.2 convolution_bitcast_fusion
  404.8 152.6 %all-reduce.3.cloned.1.call-done = (f32[3,3,512]{2,0,1:T(4,128)}, f32[16,512]{1,0:T(8,128)}, f32[16,512]{1,0:T(8,128)}) async-done(((f32[3,3,512]{2,0,1:T(4,128)}, f32[16,512]{1,0:T(8,128)}, f32[16,512]{1,0:T(8,128)}), (f32[3,3,512]{2,0,1:T(4,128)}, f32[16,512]{1,0:T(8,128)}, f32[16,512]{1,0:T(8,128)})) %all-reduce.3.cloned.1.call-update) | async-done | bytes 83984 | tf_op jit(solution)/shard_map/psum | solution.py:118
  558.8 299.8 %reduce-scatter.2.cloned.1.call-done = f32[512,512]{0,1:T(8,128)} async-done(((f32[8192,512]{0,1:T(8,128)}), f32[512,512]{0,1:T(8,128)}) %reduce-scatter.2.cloned.1.call-update) | async-done | bytes 1048592 | tf_op jit(solution)/shard_map/reduce_scatter | solution.py:120
  (272 shorter events, 85.0 us)
Async XLA Ops:
  7.2 60.9 %all-gather.4.cloned.1.call-start = ((), (), s32[]{:S(2)}) async-start(), calls=%async_computation.1 | async-start | bytes 2228224 | tf_op jit(solution)/shard_map/all_gather | solution.py:60
  7.9 180.5 %all-gather.6.cloned.1.call-start = ((), (), s32[]{:S(2)}) async-start(), calls=%async_computation.3 | async-start | bytes 8912896 | tf_op jit(solution)/shard_map/all_gather | solution.py:65
  8.6 548.8 %all-reduce.3.cloned.1.call-start = ((), (), s32[]{:S(2)}) async-start(), calls=%async_computation.4 | async-start | bytes 180224 | tf_op jit(solution)/shard_map/psum | solution.py:118
  9.4 50.9 %collective-permute-start = (bf16[3,2,512]{2,1,0:T(2,128)(2,1)S(1)}, bf16[3,2,512]{2,1,0:T(2,128)(2,1)S(1)}, u32[]{:S(2)}, u32[]{:S(2)}) collective-permute-start(bf16[3,2,512]{2,1,0:T(2,128)(2,1)S(1)} %slice.248), channel_id=1, source_target_pairs={{0,16},{16,32},{32,48},{48,64},{64,80},{80,96},{96,112},{112,128},... | collective-permute-start | bytes 18440 | tf_op jit(solution)/shard_map/ppermute | solution.py:11
  17.0 44.8 %copy-start.40 = (f32[3,512]{1,0:T(4,128)}, f32[3,512]{1,0:T(4,128)S(1)}, u32[]{:S(2)}) copy-start(f32[3,512]{1,0:T(4,128)S(1)} %get-tuple-element.514) | copy-start | bytes 18436
  17.0 44.9 %copy-start.42 = (f32[3,512]{1,0:T(4,128)}, f32[3,512]{1,0:T(4,128)S(1)}, u32[]{:S(2)}) copy-start(f32[3,512]{1,0:T(4,128)S(1)} %get-tuple-element.515) | copy-start | bytes 18436
  62.0 6.0 copy-start.7
  62.2 5.9 copy-start.13
  62.2 5.9 copy-start.19
  62.2 5.9 copy-start.23
  62.3 5.9 copy-start.27
  62.3 5.8 copy-start.29
  62.3 5.8 copy-start.35
  62.3 5.8 copy-start.46
  62.4 5.8 copy-start.9
  62.4 5.8 copy-start.11
  62.4 5.7 copy-start.17
  62.5 5.7 copy-start.21
  62.5 5.7 copy-start.25
  62.5 5.7 copy-start.31
  62.5 5.7 copy-start.37
  62.5 5.7 copy-start.48
  68.0 128.1 %copy-start.33 = (f32[16,512]{1,0:T(8,128)S(1)}, f32[16,512]{1,0:T(8,128)}, u32[]{:S(2)}) copy-start(f32[16,512]{1,0:T(8,128)} %param.18) | copy-start | bytes 98308
  196.8 5.3 copy-start
  223.0 24.5 %copy-start.8 = (f32[4,1,1,512]{3,0,1,2:T(4,128)S(1)}, f32[4,1,1,512]{3,0,1,2:T(4,128)}, u32[]{:S(2)}) copy-start(f32[4,1,1,512]{3,0,1,2:T(4,128)} %copy-done.7) | copy-start | bytes 24580
  224.7 24.6 %copy-start.14 = (f32[4,1,1,512]{3,0,1,2:T(4,128)S(1)}, f32[4,1,1,512]{3,0,1,2:T(4,128)}, u32[]{:S(2)}) copy-start(f32[4,1,1,512]{3,0,1,2:T(4,128)} %copy-done.13) | copy-start | bytes 24580
  226.3 23.8 %copy-start.20 = (f32[4,1,1,512]{3,0,1,2:T(4,128)S(1)}, f32[4,1,1,512]{3,0,1,2:T(4,128)}, u32[]{:S(2)}) copy-start(f32[4,1,1,512]{3,0,1,2:T(4,128)} %copy-done.19) | copy-start | bytes 24580
  226.3 24.6 %copy-start.24 = (f32[4,1,1,512]{3,0,1,2:T(4,128)S(1)}, f32[4,1,1,512]{3,0,1,2:T(4,128)}, u32[]{:S(2)}) copy-start(f32[4,1,1,512]{3,0,1,2:T(4,128)} %copy-done.23) | copy-start | bytes 24580
  228.0 23.7 %copy-start.28 = (f32[4,1,1,512]{3,0,1,2:T(4,128)S(1)}, f32[4,1,1,512]{3,0,1,2:T(4,128)}, u32[]{:S(2)}) copy-start(f32[4,1,1,512]{3,0,1,2:T(4,128)} %copy-done.27) | copy-start | bytes 24580
  229.5 22.9 %copy-start.30 = (f32[4,1,1,512]{3,0,1,2:T(4,128)S(1)}, f32[4,1,1,512]{3,0,1,2:T(4,128)}, u32[]{:S(2)}) copy-start(f32[4,1,1,512]{3,0,1,2:T(4,128)} %copy-done.29) | copy-start | bytes 24580
  229.5 23.7 %copy-start.36 = (f32[4,1,1,512]{3,0,1,2:T(4,128)S(1)}, f32[4,1,1,512]{3,0,1,2:T(4,128)}, u32[]{:S(2)}) copy-start(f32[4,1,1,512]{3,0,1,2:T(4,128)} %copy-done.35) | copy-start | bytes 24580
  231.2 22.8 %copy-start.47 = (f32[4,1,1,512]{3,0,1,2:T(4,128)S(1)}, f32[4,1,1,512]{3,0,1,2:T(4,128)}, u32[]{:S(2)}) copy-start(f32[4,1,1,512]{3,0,1,2:T(4,128)} %copy-done.46) | copy-start | bytes 24580
  237.7 20.9 %copy-start.10 = (f32[4,1,1,512]{3,0,1,2:T(4,128)S(1)}, f32[4,1,1,512]{3,0,1,2:T(4,128)}, u32[]{:S(2)}) copy-start(f32[4,1,1,512]{3,0,1,2:T(4,128)} %copy-done.9) | copy-start | bytes 24580
  239.3 20.1 %copy-start.12 = (f32[4,1,1,512]{3,0,1,2:T(4,128)S(1)}, f32[4,1,1,512]{3,0,1,2:T(4,128)}, u32[]{:S(2)}) copy-start(f32[4,1,1,512]{3,0,1,2:T(4,128)} %copy-done.11) | copy-start | bytes 24580
  239.3 20.8 %copy-start.18 = (f32[4,1,1,512]{3,0,1,2:T(4,128)S(1)}, f32[4,1,1,512]{3,0,1,2:T(4,128)}, u32[]{:S(2)}) copy-start(f32[4,1,1,512]{3,0,1,2:T(4,128)} %copy-done.17) | copy-start | bytes 24580
  241.0 19.8 %copy-start.22 = (f32[4,1,1,512]{3,0,1,2:T(4,128)S(1)}, f32[4,1,1,512]{3,0,1,2:T(4,128)}, u32[]{:S(2)}) copy-start(f32[4,1,1,512]{3,0,1,2:T(4,128)} %copy-done.21) | copy-start | bytes 24580
  242.6 19.0 %copy-start.26 = (f32[4,1,1,512]{3,0,1,2:T(4,128)S(1)}, f32[4,1,1,512]{3,0,1,2:T(4,128)}, u32[]{:S(2)}) copy-start(f32[4,1,1,512]{3,0,1,2:T(4,128)} %copy-done.25) | copy-start | bytes 24580
  242.6 19.7 %copy-start.32 = (f32[4,1,1,512]{3,0,1,2:T(4,128)S(1)}, f32[4,1,1,512]{3,0,1,2:T(4,128)}, u32[]{:S(2)}) copy-start(f32[4,1,1,512]{3,0,1,2:T(4,128)} %copy-done.31) | copy-start | bytes 24580
  244.3 18.8 %copy-start.38 = (f32[4,1,1,512]{3,0,1,2:T(4,128)S(1)}, f32[4,1,1,512]{3,0,1,2:T(4,128)}, u32[]{:S(2)}) copy-start(f32[4,1,1,512]{3,0,1,2:T(4,128)} %copy-done.37) | copy-start | bytes 24580
  245.9 17.9 %copy-start.49 = (f32[4,1,1,512]{3,0,1,2:T(4,128)S(1)}, f32[4,1,1,512]{3,0,1,2:T(4,128)}, u32[]{:S(2)}) copy-start(f32[4,1,1,512]{3,0,1,2:T(4,128)} %copy-done.48) | copy-start | bytes 24580
  327.4 52.3 %copy-start.15 = (f32[16,512]{1,0:T(8,128)S(1)}, f32[16,512]{1,0:T(8,128)}, u32[]{:S(2)}) copy-start(f32[16,512]{1,0:T(8,128)} %get-tuple-element.504) | copy-start | bytes 98308
  327.4 52.3 %copy-start.51 = (f32[128]{0:T(128)S(1)}, f32[128]{0:T(128)}, u32[]{:S(2)}) copy-start(f32[128]{0:T(128)} %iota_add_fusion) | copy-start | bytes 1540
  385.7 8.9 %copy-start.41 = (f32[3,512]{1,0:T(4,128)S(1)}, f32[3,512]{1,0:T(4,128)}, u32[]{:S(2)}) copy-start(f32[3,512]{1,0:T(4,128)} %copy-done.40) | copy-start | bytes 18436
  385.7 8.9 %copy-start.43 = (f32[3,512]{1,0:T(4,128)S(1)}, f32[3,512]{1,0:T(4,128)}, u32[]{:S(2)}) copy-start(f32[3,512]{1,0:T(4,128)} %copy-done.42) | copy-start | bytes 18436
  385.7 8.9 %copy-start.45 = (f32[3,1,512]{2,0,1:T(4,128)S(1)}, f32[3,1,512]{2,0,1:T(4,128)}, u32[]{:S(2)}) copy-start(f32[3,1,512]{2,0,1:T(4,128)} %copy-done.44) | copy-start | bytes 18436
  388.4 8.2 copy-start.6
  388.5 6.1 collective-permute-start.1
  396.6 462.0 %reduce-scatter.2.cloned.1.call-start = ((), (), s32[]{:S(2)}) async-start(), calls=%async_computation.2 | async-start | bytes 17825792 | tf_op jit(solution)/shard_map/reduce_scatter | solution.py:120
  (11 other events, 27.0 us)
Sparse Core Ops, SparseCore 0:
  9.8 41.2 all-gather.3
  53.7 134.6 all-gather.5
  396.7 160.7 all-reduce.2
  561.4 297.0 reduce-scatter.1
where the time goes:
time: 874 us; the launch traced here: 870 us
  waiting for transfers between devices  578 us (66%)
  other arithmetic  127 us (15%)
  blocking collectives  107 us (12%)
  local copies, waits for them, and re-layouts  21.9 us (3%)
  between operations  14.8 us (2%)
  matrix products  13.5 us (2%)
    reduce_scatter x1, waiting for transfers between devices, on_device(): lax.psum_scatter(lax.dot_general(columns, y_rounded, (((0,), (0,)), ((),...  300 us
    psum x1, waiting for transfers between devices, on_device(): lax.psum((filter_part, grad_res_part, grad_rate_part), 'ctx')  153 us
    all_gather x1, waiting for transfers between devices, on_device(): lax.all_gather(out_weight, 'ctx', axis=0, tiled=True)  120 us
    all_gather x3, blocking collectives, carried_in(): everything = jax.tree.map(lambda part: lax.all_gather(part, axis), array)  107 us
    unnamed x62, other arithmetic  68.5 us
    select_n x32, other arithmetic, lap(): return jax.tree.map(lambda a, b: jnp.where(reached, a, b), new, before)  24.7 us
  transfers between devices with their start and end apart: 6, of which 4 were waited for; matrix products, arithmetic and copies ran while one was open for 3% of the time, Pallas kernels for 0%

commit v1 on v0

--- a/solution.py
+++ b/solution.py
@@ -62,7 +62,9 @@
     columns = panels
     grad_y = jnp.dot(
         columns,
-        lax.all_gather(out_weight, "ctx", axis=0, tiled=True),
+        jnp.concatenate(
+            lax.all_to_all(jnp.stack([out_weight] * lax.axis_size("ctx")), "ctx", 0, 0), axis=0
+        ),
         preferred_element_type=jnp.float32,
     )
     taps = short_filters.shape[1]

time: 874 us -> 948 us (1.085)
  blocking collectives: 107 us -> 283 us
  waiting for transfers between devices: 578 us -> 463 us
  starting transfers between devices: 7.04 us -> 18 us
    all_gather x3, blocking collectives: 107 us -> 283 us  [carried_in(): everything = jax.tree.map(lambda part: lax.all_gather(part, axis), array)]
    all_gather x1 -> x0, waiting for transfers between devices: 120 us -> none  [on_device(): lax.all_gather(out_weight, 'ctx', axis=0, tiled=True)]
    all_to_all x0 -> x1, starting transfers between devices: none -> 11.8 us  [on_device(): lax.all_to_all(jnp.stack([out_weight] * lax.axis_size('ctx')), 'ctx', 0, 0)]
  transfers between devices with their start and end apart: 6 -> 6, of which waited for: 4 -> 3; matrix products, arithmetic and copies ran while one was open for 3% -> 2% of each run, Pallas kernels for 0% -> 0%
where the time goes in v1:
time: 948 us; the launch traced here: 944 us
  waiting for transfers between devices  463 us (49%)
  blocking collectives  283 us (30%)
  other arithmetic  126 us (13%)
  local copies, waits for them, and re-layouts  25.5 us (3%)
  starting transfers between devices  18 us (2%)
  between operations  14.8 us (2%)
  matrix products  13.5 us (1%)
    reduce_scatter x1, waiting for transfers between devices, on_device(): lax.psum_scatter(lax.dot_general(columns, y_rounded, (((0,), (0,)), ((),...  300 us
    all_gather x3, blocking collectives, carried_in(): everything = jax.tree.map(lambda part: lax.all_gather(part, axis), array)  283 us
    psum x1, waiting for transfers between devices, on_device(): lax.psum((filter_part, grad_res_part, grad_rate_part), 'ctx')  159 us
    unnamed x62, other arithmetic  68.4 us
    select_n x32, other arithmetic, lap(): return jax.tree.map(lambda a, b: jnp.where(reached, a, b), new, before)  24.7 us
  transfers between devices with their start and end apart: 6, of which 3 were waited for; matrix products, arithmetic and copies ran while one was open for 2% of the time, Pallas kernels for 0%

profile of v1, /device:TPU:1, one launch (start us, length us, event | category | flops | bytes accessed | tf_op | source)
XLA Modules:
  0.0 944.1 jit_solution(2859764580392363595)
XLA Ops:
  7.2 5.2 stack.19
  12.3 11.8 %all-to-all-start = ((bf16[16,512,512]{2,1,0:T(8,128)(2,1)}), bf16[16,512,512]{2,1,0:T(8,128)(2,1)}, u32[]{:S(2)}, u32[]{:S(2)}) async-start(bf16[16,512,512]{2,1,0:T(8,128)(2,1)} %stack.19), calls=%async_computation.1 | async-start | bytes 16777216 | tf_op jit(solution)/shard_map/all_to_all | solution.py:66
  24.2 4.7 collective-permute-start
  30.9 214.9 %all-gather = f32[256,512]{1,0:T(8,128)} all-gather(f32[16,512]{1,0:T(8,128)S(1)} %get-tuple-element.508), channel_id=2, replica_groups=mesh['ctx'=16,'fsdp'=16] {'ctx'}, dimensions={0}, use_global_device_ids=true | all-gather | bytes 557056 | tf_op jit(solution)/shard_map/all_gather | solution.py:16
  245.8 1.8 broadcast_power_fusion
  255.3 5.3 fusion.8
  269.0 1.6 constant_dynamic-update-slice_fusion.60
  270.6 1.7 constant_dynamic-update-slice_fusion.59
  272.3 1.6 constant_dynamic-update-slice_fusion.58
  273.8 1.7 constant_dynamic-update-slice_fusion.57
  277.1 1.7 constant_dynamic-update-slice_fusion.55
  278.7 1.6 constant_dynamic-update-slice_fusion.54
  280.3 1.7 constant_dynamic-update-slice_fusion.53
  283.5 1.7 constant_dynamic-update-slice_fusion.51
  286.7 1.7 constant_dynamic-update-slice_fusion.49
  290.0 1.7 constant_dynamic-update-slice_fusion.47
  291.6 1.6 constant_dynamic-update-slice_fusion.46
  293.2 1.7 constant_dynamic-update-slice_fusion.45
  294.9 1.6 constant_dynamic-update-slice_fusion.44
  296.5 1.7 constant_dynamic-update-slice_fusion.43
  298.1 1.6 constant_dynamic-update-slice_fusion.42
  299.7 1.7 constant_dynamic-update-slice_fusion.41
  301.4 1.6 constant_dynamic-update-slice_fusion.40
  303.0 1.6 constant_dynamic-update-slice_fusion.39
  304.6 1.6 constant_dynamic-update-slice_fusion.38
  306.2 1.7 constant_dynamic-update-slice_fusion.37
  307.9 1.6 constant_dynamic-update-slice_fusion.36
  309.5 1.7 constant_dynamic-update-slice_fusion.35
  311.2 1.6 constant_dynamic-update-slice_fusion.34
  312.7 1.7 constant_dynamic-update-slice_fusion.33
  314.4 1.7 constant_dynamic-update-slice_fusion.32
  321.7 1.7 constant_dynamic-update-slice_fusion.31
  332.1 5.6 while.58
  337.7 7.2 multiply_add_fusion.1
  346.9 2.0 copy-done.5
  349.0 35.9 %all_gather.19 = f32[16,16,512]{2,1,0:T(8,128)S(1)} all-gather(f32[1,16,512]{2,1,0:T(8,128)S(1)} %slice.365), channel_id=1, replica_groups=mesh['ctx'=16,'fsdp'=16] {'ctx'}, dimensions={0}, use_global_device_ids=true | all-gather | bytes 557056 | tf_op jit(solution)/shard_map/all_gather | solution.py:16
  384.8 12.7 %while.57 = (s32[]{:T(128)}, f32[16,512]{1,0:T(8,128)S(1)}, s32[]{:T(128)}, f32[16,16,512]{2,1,0:T(8,128)}, f32[16,16,512]{2,1,0:T(8,128)S(1)}, /*index=5*/s32[]{:T(128)}, s32[]{:T(128)}) while((s32[]{:T(128)}, f32[16,512]{1,0:T(8,128)S(1)}, s32[]{:T(128)}, f32[16,16,512]{2,1,0:T(8,128)}, f32[16,16,512]{2,1,0:T(8,128)S(1)}, ...), condition=%wide.region_3.4_spmd.clone, body=%wide.region_2.3_spmd.clone.sunk | while | flops 32772 | bytes 131173 | solution.py:29
  397.6 2.6 copy.25
  400.2 2.1 copy-done.3
  402.3 32.0 %all_gather.21 = f32[16,16,512]{2,1,0:T(8,128)S(1)} all-gather(f32[1,16,512]{2,1,0:T(8,128)S(1)} %slice.398), channel_id=1, replica_groups=mesh['ctx'=16,'fsdp'=16] {'ctx'}, dimensions={0}, use_global_device_ids=true | all-gather | bytes 557056 | tf_op jit(solution)/shard_map/all_gather | solution.py:16
  434.3 12.8 %while.59 = (s32[]{:T(128)}, f32[16,512]{1,0:T(8,128)S(1)}, s32[]{:T(128)}, f32[16,16,512]{2,1,0:T(8,128)}, f32[16,16,512]{2,1,0:T(8,128)S(1)}, /*index=5*/s32[]{:T(128)}, s32[]{:T(128)}, s32[]{:T(128)}, s32[]{:T(128)}) while((s32[]{:T(128)}, f32[16,512]{1,0:T(8,128)S(1)}, s32[]{:T(128)}, f32[16,16,512]{2,1,0:T(8,128)}, ...), condition=%wide.region_9.10_spmd.clone, body=%wide.region_8.9_spmd.clone.sunk | while | flops 32776 | bytes 131235 | solution.py:29
  447.1 3.1 slice_add_fusion
  450.6 2.3 fusion.2
  453.2 2.5 multiply_reduce_fusion
  458.0 4.0 collective-permute-done.1
  464.1 8.2 convolution_bitcast_fusion
  472.3 159.0 %all-reduce.3.cloned.1.call-done = (f32[3,3,512]{2,0,1:T(4,128)}, f32[16,512]{1,0:T(8,128)}, f32[16,512]{1,0:T(8,128)}) async-done(((f32[3,3,512]{2,0,1:T(4,128)}, f32[16,512]{1,0:T(8,128)}, f32[16,512]{1,0:T(8,128)}), (f32[3,3,512]{2,0,1:T(4,128)}, f32[16,512]{1,0:T(8,128)}, f32[16,512]{1,0:T(8,128)})) %all-reduce.3.cloned.1.call-update) | async-done | bytes 83984 | tf_op jit(solution)/shard_map/psum | solution.py:120
  632.6 299.9 %reduce-scatter.2.cloned.1.call-done = f32[512,512]{0,1:T(8,128)} async-done(((f32[8192,512]{0,1:T(8,128)}), f32[512,512]{0,1:T(8,128)}) %reduce-scatter.2.cloned.1.call-update) | async-done | bytes 1048592 | tf_op jit(solution)/shard_map/reduce_scatter | solution.py:122
  (278 shorter events, 81.7 us)
Async XLA Ops:
  12.3 11.8 %copy-start.21 = (bf16[3,128,512]{2,1,0:T(8,128)(2,1)S(1)}, bf16[3,128,512]{2,1,0:T(8,128)(2,1)}, u32[]{:S(2)}) copy-start(bf16[3,128,512]{2,1,0:T(8,128)(2,1)} %param.16) | copy-start | bytes 1179652
  12.3 17.8 %copy-start.53 = (f32[3,3,512]{2,1,0:T(4,128)S(1)}, f32[3,3,512]{2,1,0:T(4,128)}, u32[]{:S(2)}) copy-start(f32[3,3,512]{2,1,0:T(4,128)} %param.17) | copy-start | bytes 55300
  12.3 17.9 %copy-start.40 = (f32[16,512]{1,0:T(8,128)S(1)}, f32[16,512]{1,0:T(8,128)}, u32[]{:S(2)}) copy-start(f32[16,512]{1,0:T(8,128)} %param.19) | copy-start | bytes 98308
  12.3 242.4 %all-to-all-start = ((bf16[16,512,512]{2,1,0:T(8,128)(2,1)}), bf16[16,512,512]{2,1,0:T(8,128)(2,1)}, u32[]{:S(2)}, u32[]{:S(2)}) async-start(bf16[16,512,512]{2,1,0:T(8,128)(2,1)} %stack.19), calls=%async_computation.1 | async-start | bytes 16777216 | tf_op jit(solution)/shard_map/all_to_all | solution.py:66
  24.1 230.6 %all-gather.3.cloned.1.call-start = ((), (), s32[]{:S(2)}) async-start(), calls=%async_computation.2 | async-start | bytes 2228224 | tf_op jit(solution)/shard_map/all_gather | solution.py:60
  24.2 224.0 %collective-permute-start = (bf16[3,2,512]{2,1,0:T(2,128)(2,1)S(1)}, bf16[3,2,512]{2,1,0:T(2,128)(2,1)S(1)}, u32[]{:S(2)}, u32[]{:S(2)}) collective-permute-start(bf16[3,2,512]{2,1,0:T(2,128)(2,1)S(1)} %slice.248), channel_id=1, source_target_pairs={{0,16},{16,32},{32,48},{48,64},{64,80},{80,96},{96,112},{112,128},... | collective-permute-start | bytes 18440 | tf_op jit(solution)/shard_map/ppermute | solution.py:11
  28.9 602.4 %all-reduce.3.cloned.1.call-start = ((), (), s32[]{:S(2)}) async-start(), calls=%async_computation.4 | async-start | bytes 180224 | tf_op jit(solution)/shard_map/psum | solution.py:120
  30.2 218.5 %copy-start.42 = (f32[3,512]{1,0:T(4,128)}, f32[3,512]{1,0:T(4,128)S(1)}, u32[]{:S(2)}) copy-start(f32[3,512]{1,0:T(4,128)S(1)} %get-tuple-element.514) | copy-start | bytes 18436
  30.2 218.5 %copy-start.44 = (f32[3,512]{1,0:T(4,128)}, f32[3,512]{1,0:T(4,128)S(1)}, u32[]{:S(2)}) copy-start(f32[3,512]{1,0:T(4,128)S(1)} %get-tuple-element.515) | copy-start | bytes 18436
  248.9 5.9 copy-start.7
  249.0 5.7 copy-start.13
  249.0 5.7 copy-start.19
  249.0 5.7 copy-start.24
  249.1 5.7 copy-start.28
  249.1 5.7 copy-start.30
  249.1 5.7 copy-start.36
  249.1 5.7 copy-start.48
  249.2 5.6 copy-start.9
  249.2 5.6 copy-start.11
  249.2 5.6 copy-start.17
  249.3 5.6 copy-start.22
  249.3 5.6 copy-start.26
  249.3 5.5 copy-start.32
  255.3 7.8 copy-start.34
  290.0 24.5 %copy-start.8 = (f32[4,1,1,512]{3,0,1,2:T(4,128)S(1)}, f32[4,1,1,512]{3,0,1,2:T(4,128)}, u32[]{:S(2)}) copy-start(f32[4,1,1,512]{3,0,1,2:T(4,128)} %copy-done.7) | copy-start | bytes 24580
  291.6 24.5 %copy-start.14 = (f32[4,1,1,512]{3,0,1,2:T(4,128)S(1)}, f32[4,1,1,512]{3,0,1,2:T(4,128)}, u32[]{:S(2)}) copy-start(f32[4,1,1,512]{3,0,1,2:T(4,128)} %copy-done.13) | copy-start | bytes 24580
  293.2 23.7 %copy-start.20 = (f32[4,1,1,512]{3,0,1,2:T(4,128)S(1)}, f32[4,1,1,512]{3,0,1,2:T(4,128)}, u32[]{:S(2)}) copy-start(f32[4,1,1,512]{3,0,1,2:T(4,128)} %copy-done.19) | copy-start | bytes 24580
  293.2 24.5 %copy-start.25 = (f32[4,1,1,512]{3,0,1,2:T(4,128)S(1)}, f32[4,1,1,512]{3,0,1,2:T(4,128)}, u32[]{:S(2)}) copy-start(f32[4,1,1,512]{3,0,1,2:T(4,128)} %copy-done.24) | copy-start | bytes 24580
  294.9 23.6 %copy-start.29 = (f32[4,1,1,512]{3,0,1,2:T(4,128)S(1)}, f32[4,1,1,512]{3,0,1,2:T(4,128)}, u32[]{:S(2)}) copy-start(f32[4,1,1,512]{3,0,1,2:T(4,128)} %copy-done.28) | copy-start | bytes 24580
  296.5 22.8 %copy-start.31 = (f32[4,1,1,512]{3,0,1,2:T(4,128)S(1)}, f32[4,1,1,512]{3,0,1,2:T(4,128)}, u32[]{:S(2)}) copy-start(f32[4,1,1,512]{3,0,1,2:T(4,128)} %copy-done.30) | copy-start | bytes 24580
  296.5 23.6 %copy-start.37 = (f32[4,1,1,512]{3,0,1,2:T(4,128)S(1)}, f32[4,1,1,512]{3,0,1,2:T(4,128)}, u32[]{:S(2)}) copy-start(f32[4,1,1,512]{3,0,1,2:T(4,128)} %copy-done.36) | copy-start | bytes 24580
  298.1 22.8 %copy-start.49 = (f32[4,1,1,512]{3,0,1,2:T(4,128)S(1)}, f32[4,1,1,512]{3,0,1,2:T(4,128)}, u32[]{:S(2)}) copy-start(f32[4,1,1,512]{3,0,1,2:T(4,128)} %copy-done.48) | copy-start | bytes 24580
  304.6 20.9 %copy-start.10 = (f32[4,1,1,512]{3,0,1,2:T(4,128)S(1)}, f32[4,1,1,512]{3,0,1,2:T(4,128)}, u32[]{:S(2)}) copy-start(f32[4,1,1,512]{3,0,1,2:T(4,128)} %copy-done.9) | copy-start | bytes 24580
  306.2 20.0 %copy-start.12 = (f32[4,1,1,512]{3,0,1,2:T(4,128)S(1)}, f32[4,1,1,512]{3,0,1,2:T(4,128)}, u32[]{:S(2)}) copy-start(f32[4,1,1,512]{3,0,1,2:T(4,128)} %copy-done.11) | copy-start | bytes 24580
  306.2 20.7 %copy-start.18 = (f32[4,1,1,512]{3,0,1,2:T(4,128)S(1)}, f32[4,1,1,512]{3,0,1,2:T(4,128)}, u32[]{:S(2)}) copy-start(f32[4,1,1,512]{3,0,1,2:T(4,128)} %copy-done.17) | copy-start | bytes 24580
  307.9 19.8 %copy-start.23 = (f32[4,1,1,512]{3,0,1,2:T(4,128)S(1)}, f32[4,1,1,512]{3,0,1,2:T(4,128)}, u32[]{:S(2)}) copy-start(f32[4,1,1,512]{3,0,1,2:T(4,128)} %copy-done.22) | copy-start | bytes 24580
  309.5 18.9 %copy-start.27 = (f32[4,1,1,512]{3,0,1,2:T(4,128)S(1)}, f32[4,1,1,512]{3,0,1,2:T(4,128)}, u32[]{:S(2)}) copy-start(f32[4,1,1,512]{3,0,1,2:T(4,128)} %copy-done.26) | copy-start | bytes 24580
  309.5 19.7 %copy-start.33 = (f32[4,1,1,512]{3,0,1,2:T(4,128)S(1)}, f32[4,1,1,512]{3,0,1,2:T(4,128)}, u32[]{:S(2)}) copy-start(f32[4,1,1,512]{3,0,1,2:T(4,128)} %copy-done.32) | copy-start | bytes 24580
  311.1 18.7 %copy-start.39 = (f32[4,1,1,512]{3,0,1,2:T(4,128)S(1)}, f32[4,1,1,512]{3,0,1,2:T(4,128)}, u32[]{:S(2)}) copy-start(f32[4,1,1,512]{3,0,1,2:T(4,128)} %copy-done.38) | copy-start | bytes 24580
  312.7 17.9 %copy-start.51 = (f32[4,1,1,512]{3,0,1,2:T(4,128)S(1)}, f32[4,1,1,512]{3,0,1,2:T(4,128)}, u32[]{:S(2)}) copy-start(f32[4,1,1,512]{3,0,1,2:T(4,128)} %copy-done.50) | copy-start | bytes 24580
  397.5 49.6 %copy-start.15 = (f32[16,512]{1,0:T(8,128)S(1)}, f32[16,512]{1,0:T(8,128)}, u32[]{:S(2)}) copy-start(f32[16,512]{1,0:T(8,128)} %get-tuple-element.504) | copy-start | bytes 98308
  397.6 49.6 %copy-start.54 = (f32[128]{0:T(128)S(1)}, f32[128]{0:T(128)}, u32[]{:S(2)}) copy-start(f32[128]{0:T(128)} %iota_add_fusion) | copy-start | bytes 1540
  453.1 9.0 copy-start.43
  453.1 9.0 copy-start.45
  453.1 9.0 copy-start.47
  455.8 8.2 copy-start.6
  455.9 6.1 collective-permute-start.1
  464.0 468.5 %reduce-scatter.2.cloned.1.call-start = ((), (), s32[]{:S(2)}) async-start(), calls=%async_computation.3 | async-start | bytes 17825792 | tf_op jit(solution)/shard_map/reduce_scatter | solution.py:122
  (14 other events, 42.4 us)
Sparse Core Ops, SparseCore 0:
  29.0 36.3 all-gather.2
  464.1 167.1 all-reduce.2
  635.4 297.0 reduce-scatter.1
